TPU v7x, 32 devices: a whole 2x2x4 slice. The times are simulated.
32 devices in a mesh: seg: 4 (over y, x), sec: 8 (over z, core).
Axes of the slice: x: 2, y: 2, z: 4, core: 2. Of those that a mesh axis runs over, the one named last changes fastest.
Arguments:
- left_env: bfloat16 [4, 8, 13, 512, 512], P('seg', 'sec'), may hold values from -0.25 to 0.25
- right_env: bfloat16 [4, 8, 13, 512, 512], P('seg', 'sec'), may hold values from -0.25 to 0.25
- left_block: bfloat16 [4, 8, 512, 512], P('seg', 'sec'), may hold values from -8 to 8
- right_block: bfloat16 [4, 8, 512, 512], P('seg', 'sec'), may hold values from -0.25 to 0.25
- inv_sv: bfloat16 [4, 8, 512], P('seg', 'sec'), may hold values from 0.5 to 2
- precond: float32 [4, 8, 512, 512], P('seg', 'sec'), may hold values from 1 to 4
- sector_dims: int32 [4, 8, 2], P('seg', 'sec'), may hold values from 128 to 512, as said below
- channel_charge: int32 [13], replicated, may hold values from -1 to 1
Outputs:
- next_vector: bfloat16 [4, 8, 512, 512], P('seg', 'sec')
- last_image: float32 [4, 8, 512, 512], P('seg', 'sec')
- projected: float32 [4, 4, 4], P('seg')
Inputs may be any that keep to these rules, and one draw needn't show every extreme that they name: `sector_dims`: in every segment some sector has left bond dimension 512 and some sector has right bond dimension 512.
All inputs are finite; a program needn't handle non-finite values.
Results may differ from a plain program's by a relative error of at most 0.024.
Values may be sent and summed in bfloat16 or wider, within the bound.
A program may use at most 64 MiB of HBM per device.

v0:
```python
import functools

import jax
import jax.numpy as jnp
from jax import lax
from jax.experimental import pallas as pl
from jax.experimental.pallas import tpu as pltpu
from jax.sharding import PartitionSpec as P

MATVECS = 4
EPS = 1e-06
ROWS = 256
COLS = 256
CHUNK = 32
BLOCK = 64
MESH = pl.DeviceIdType.MESH


def fold(values):
    rows, columns = values.shape
    block = jnp.sum(values.reshape(rows // 8, 8, columns), axis=0)
    total = block[:, :128]
    for at in range(128, columns, 128):
        total = total + block[:, at : at + 128]
    return total


def kernel(
    segs, secs,
    charge_ref, dims_ref, left_hbm, right_hbm, block_hbm, other_hbm, inv_ref, precond_hbm,
    next_ref, image_ref, projected_ref,
    left_ref, right_ref, block_ref, precond_ref, nb_ref, ninv_ref, scaled_ref, pinv_ref, basis_ref, lx_ref, prefix_ref,
    stay_ref, up_out, low_out, up_in, low_in, slots_ref, rows_ref, gram_ref, proj_ref, order_ref,
    load_sem, guess_send, guess_recv, halo_send, halo_recv, sum_send, sum_recv,
):
    channels, width, _ = left_ref.shape
    tiles = width // ROWS
    halves = width // COLS
    pieces = tiles * halves
    count = secs * width * width
    f32, bf16 = jnp.float32, jnp.bfloat16
    seg, sec = lax.axis_index("seg"), lax.axis_index("sec")
    seg_before = lax.rem(seg + segs - 1, segs)
    seg_after = lax.rem(seg + 1, segs)

    load_left = pltpu.make_async_copy(left_hbm, left_ref, load_sem.at[0])
    load_right = pltpu.make_async_copy(right_hbm, right_ref, load_sem.at[1])
    load_block = pltpu.make_async_copy(block_hbm, block_ref, load_sem.at[2])
    load_precond = pltpu.make_async_copy(precond_hbm, precond_ref, load_sem.at[3])
    load_precond.start()
    load_block.start()
    load_left.start()
    load_right.start()

    barrier = pltpu.get_barrier_semaphore()
    pl.semaphore_signal(barrier, inc=1, device_id=(seg_before, sec), device_id_type=MESH)
    pl.semaphore_signal(barrier, inc=1, device_id=(seg_after, sec), device_id_type=MESH)
    for offset in range(1, secs):
        peer = lax.rem(sec + offset, secs)
        pl.semaphore_signal(barrier, inc=1, device_id=(seg, peer), device_id_type=MESH)
    pl.semaphore_wait(barrier, secs + 1)

    def remote(src, dst, send, recv, device):
        return pltpu.make_async_remote_copy(
            src_ref=src, dst_ref=dst, send_sem=send, recv_sem=recv,
            device_id=device, device_id_type=MESH,
        )

    send_inv = remote(
        inv_ref, ninv_ref, guess_send.at[0], guess_recv.at[0], (seg_before, sec)
    )
    send_block = remote(
        other_hbm, nb_ref, guess_send.at[1], guess_recv.at[1], (seg_before, sec)
    )
    send_inv.start()
    send_block.start()

    keys = []
    for w in range(channels):
        q = charge_ref[w]
        keys.append(jnp.where(q == 1, 0, jnp.where(q == -1, 1, 2)))
    raising = jnp.int32(0)
    moving = jnp.int32(0)
    for w in range(channels):
        raising = raising + jnp.where(keys[w] == 0, 1, 0)
        moving = moving + jnp.where(keys[w] <= 1, 1, 0)
    places = []
    for w in range(channels):
        place = jnp.int32(0)
        for v in range(channels):
            if v < w:
                place = place + jnp.where(keys[v] <= keys[w], 1, 0)
            elif v > w:
                place = place + jnp.where(keys[v] < keys[w], 1, 0)
        places.append(place)
    for i in range(channels):
        who = jnp.int32(0)
        for w in range(channels):
            who = who + jnp.where(places[w] == i, w, 0)
        order_ref[i] = who

    load_precond.wait()
    gram_ref[...] = jnp.zeros_like(gram_ref)
    rows_ref[...] = jnp.zeros_like(rows_ref)
    proj_ref[...] = jnp.zeros_like(proj_ref)

    @pl.loop(0, width // CHUNK)
    def _(c):
        at = pl.ds(pl.multiple_of(c * CHUNK, CHUNK), CHUNK)
        pinv_ref[at, :] = 1.0 / precond_ref[at, :]
        for k in range(1, MATVECS):
            basis_ref[k, at, :] = jnp.zeros((CHUNK, width), bf16)

    @pl.loop(0, ROWS // CHUNK)
    def _(c):
        at = pl.ds(pl.multiple_of(c * CHUNK, CHUNK), CHUNK)
        prefix_ref[0, at, :] = jnp.zeros((CHUNK, COLS), f32)

    @pl.when(sec == 0)
    def _():
        @pl.loop(0, MATVECS * pieces)
        def _(n):
            up_in[n] = jnp.zeros((ROWS, COLS), bf16)

    @pl.when(sec == secs - 1)
    def _():
        @pl.loop(0, MATVECS * pieces)
        def _(n):
            low_in[n] = jnp.zeros((ROWS, COLS), bf16)

    def masked(values, start, left=0):
        row = start + lax.broadcasted_iota(jnp.int32, values.shape, 0)
        column = left + lax.broadcasted_iota(jnp.int32, values.shape, 1)
        inside = (row < dims_ref[0]) & (column < dims_ref[1])
        return jnp.where(inside, values, 0.0)

    def sum_copies(r):
        own = slots_ref.at[r, sec]
        return [
            remote(
                own, own, sum_send.at[r], sum_recv.at[r],
                (seg, lax.rem(sec + offset, secs)),
            )
            for offset in range(1, secs)
        ]

    def total(r, tile):
        slots_ref[r, sec] = tile
        for copy in sum_copies(r):
            copy.start()
        arrived = slots_ref.at[r, pl.ds(0, secs - 1)]
        pltpu.make_async_copy(arrived, arrived, sum_recv.at[r]).wait()
        return jnp.sum(slots_ref[r], axis=0) * (1.0 / count)

    send_inv.wait_recv()
    load_block.wait()
    scaled_ref[...] = (
        block_ref[...].astype(f32) * ninv_ref[...].astype(f32)
    ).astype(bf16)
    send_block.wait_recv()

    @pl.loop(0, tiles)
    def _(t):
        at = pl.ds(pl.multiple_of(t * ROWS, ROWS), ROWS)
        image_ref[at, :] = masked(
            jnp.dot(scaled_ref[at, :], nb_ref[...], preferred_element_type=f32), t * ROWS
        )

    def square(c, carry):
        part = image_ref[pl.ds(pl.multiple_of(c * CHUNK, CHUNK), CHUNK), :]
        return carry + fold(part * part)

    guess_sq = lax.fori_loop(0, width // CHUNK, square, jnp.zeros((8, 128), f32))
    rows_ref[19:20, :] = jnp.sum(guess_sq, axis=0, keepdims=True)

    @pl.loop(0, width // CHUNK)
    def _(c):
        at = pl.ds(pl.multiple_of(c * CHUNK, CHUNK), CHUNK)
        basis_ref[0, at, :] = image_ref[at, :].astype(bf16)

    load_left.wait()
    load_right.wait()

    def up_copy(n):
        return remote(
            up_out.at[n], up_in.at[n], halo_send.at[0, n], halo_recv.at[0, n],
            (seg, lax.rem(sec + 1, secs)),
        )

    def low_copy(n):
        return remote(
            low_out.at[n], low_in.at[n], halo_send.at[1, n], halo_recv.at[1, n],
            (seg, lax.rem(sec + secs - 1, secs)),
        )

    @pl.loop(0, MATVECS)
    def _(k):
        def process(kk, piece, carry):
            t, h = divmod(piece, halves)
            n = k * pieces + piece
            across = pl.ds(h * COLS, COLS)

            @pl.when(sec > 0)
            def _():
                up_copy(n).wait_recv()

            @pl.when(sec < secs - 1)
            def _():
                low_copy(n).wait_recv()

            def body(c, carry):
                inner = pl.ds(pl.multiple_of(c * BLOCK, BLOCK), BLOCK)
                start = t * ROWS + c * BLOCK
                at = pl.ds(pl.multiple_of(start, BLOCK), BLOCK)
                image = stay_ref[at, across] + up_in[n, inner, :].astype(f32)
                image = masked(image + low_in[n, inner, :].astype(f32), start, h * COLS)
                image_ref[at, across] = image
                pinv = pinv_ref[at, across]
                lifted = image * pinv
                new = []
                for j in range(kk + 1):
                    vector = basis_ref[j, at, across].astype(f32)
                    new.append(fold(vector * image))
                    new.append(fold(vector * lifted))
                new.append(fold(lifted * lifted))
                lifted_x = basis_ref[k, at, across].astype(f32) * pinv
                new.append(fold(lifted * lifted_x))
                return tuple(a + b for a, b in zip(carry, new))

            return lax.fori_loop(0, ROWS // BLOCK, body, carry)

        for t in range(tiles):
            rows = pl.ds(t * ROWS, ROWS)
            vector = basis_ref[k]
            for w in range(channels):
                lx_ref[w] = jnp.dot(
                    left_ref[w, rows, :], vector, preferred_element_type=f32
                ).astype(bf16)
            for h in range(halves):
                n = k * pieces + t * halves + h
                across = pl.ds(h * COLS, COLS)
                for i in range(channels):
                    w = order_ref[i]
                    term = lax.dot_general(
                        lx_ref[w], right_ref[w, across, :], (((1,), (1,)), ((), ())),
                        preferred_element_type=f32,
                    )
                    prefix_ref[i + 1] = prefix_ref[i] + term
                first = prefix_ref[raising]
                second = prefix_ref[moving]
                up_out[n] = first.astype(bf16)
                low_out[n] = (second - first).astype(bf16)

                @pl.when(sec < secs - 1)
                def _():
                    up_copy(n).start()

                @pl.when(sec > 0)
                def _():
                    low_copy(n).start()

                stay_ref[rows, across] = prefix_ref[channels] - second

        def put(row, value):
            rows_ref[row : row + 1, :] = jnp.sum(value, axis=0, keepdims=True)

        def reduce(kk):
            def own(c, carry):
                at = pl.ds(pl.multiple_of(c * CHUNK, CHUNK), CHUNK)
                current = basis_ref[kk, at, :].astype(f32)
                lifted = current * pinv_ref[at, :]
                new = []
                for j in range(kk + 1):
                    vector = basis_ref[j, at, :].astype(f32)
                    new.append(fold(vector * current))
                    new.append(fold(vector * lifted))
                new.append(fold(lifted * lifted))
                return tuple(a + b for a, b in zip(carry, new))

            zero = jnp.zeros((8, 128), f32)
            own_carry = lax.fori_loop(0, width // CHUNK, own, (zero,) * (2 * kk + 3))
            carry = (zero,) * (2 * kk + 4)
            for piece in range(pieces):
                carry = process(kk, piece, carry)
            for j in range(kk + 1):
                put(j, carry[2 * j])
                put(4 + j, own_carry[2 * j])
                put(8 + j, carry[2 * j + 1])
                put(12 + j, own_carry[2 * j + 1])
            put(16, carry[2 * kk + 2])
            put(17, carry[2 * kk + 3])
            put(18, own_carry[2 * kk + 2])

        for kk in range(MATVECS):
            pl.when(k == kk)(functools.partial(reduce, kk))

        sums = jnp.sum(rows_ref[...], axis=1, keepdims=True)
        lane = lax.broadcasted_iota(jnp.int32, (8, 128), 1)
        tile = jnp.where(
            lane == 0, sums[0:8], jnp.where(lane == 1, sums[8:16], sums[16:24])
        )
        tile = total(k, tile)

        def entry(source, row, at):
            return source[row : row + 1, at : at + 1]

        guess_scale = lax.rsqrt(entry(tile, 3, 2) + EPS)
        factor = jnp.where(k == 0, guess_scale, 1.0)
        tile = tile * (factor * factor)
        gram_ref[k] = tile
        proj_ref[...] = jnp.where(lane == k, tile[:, 0:1], proj_ref[...])

        row = lax.broadcasted_iota(jnp.int32, (8, 128), 0)
        theta = jnp.sum(
            jnp.where((row == k) & (lane == 0), tile, 0.0), axis=(0, 1), keepdims=True
        )
        weights = [
            entry(tile, j, 1) - theta * entry(tile, 4 + j, 1) for j in range(MATVECS)
        ]
        norm_sq = (
            entry(tile, 0, 2) - 2.0 * theta * entry(tile, 1, 2)
            + theta * theta * entry(tile, 2, 2)
        )
        for i in range(MATVECS):
            column = gram_ref[i]
            inner = weights[i] * entry(column, 4 + i, 0) - 2.0 * weights[i]
            for j in range(i):
                inner = inner + 2.0 * weights[j] * entry(column, 4 + j, 0)
            norm_sq = norm_sq + weights[i] * inner
        scale = lax.rsqrt(jnp.maximum(norm_sq, 0.0) + EPS)

        @pl.when(k == 0)
        def _():
            @pl.loop(0, width // CHUNK)
            def _(c):
                at = pl.ds(pl.multiple_of(c * CHUNK, CHUNK), CHUNK)
                basis_ref[0, at, :] = (basis_ref[0, at, :].astype(f32) * guess_scale).astype(bf16)

        def update(kk):
            @pl.loop(0, width // CHUNK)
            def _(c):
                at = pl.ds(pl.multiple_of(c * CHUNK, CHUNK), CHUNK)
                image = image_ref[at, :]
                if kk == 0:
                    image = image * factor
                current = basis_ref[kk, at, :].astype(f32)
                remain = (image - theta * current) * pinv_ref[at, :]
                for j in range(kk + 1):
                    remain = remain - weights[j] * basis_ref[j, at, :].astype(f32)
                basis_ref[kk + 1, at, :] = (remain * scale).astype(bf16)

        for kk in range(MATVECS):
            pl.when(k == kk)(functools.partial(update, kk))

    @pl.loop(0, width // CHUNK)
    def _(c):
        at = pl.ds(pl.multiple_of(c * CHUNK, CHUNK), CHUNK)
        next_ref[at, :] = basis_ref[MATVECS, at, :]

    projected_ref[...] = proj_ref[:MATVECS, :MATVECS]

    send_inv.wait_send()
    send_block.wait_send()

    @pl.when(sec < secs - 1)
    def _():
        @pl.loop(0, MATVECS * pieces)
        def _(n):
            up_copy(n).wait_send()

    @pl.when(sec > 0)
    def _():
        @pl.loop(0, MATVECS * pieces)
        def _(n):
            low_copy(n).wait_send()

    @pl.loop(0, MATVECS)
    def _(r):
        sent = slots_ref.at[r, pl.ds(0, secs - 1)]
        pltpu.make_async_copy(sent, sent, sum_send.at[r]).wait()


def finish(next_in, image_in, projected_in, next_ref, image_ref, projected_ref):
    next_ref[...] = next_in[...]
    image_ref[...] = image_in[...]
    projected_ref[...] = projected_in[...]


def per_device(
    left_env, right_env, left_block, right_block, inv_sv, precond, sector_dims, channel_charge
):
    segs, secs = lax.axis_size("seg"), lax.axis_size("sec")
    channels, width = left_env.shape[2], left_env.shape[-1]
    halos = MATVECS * (width // ROWS) * (width // COLS)
    f32, bf16 = jnp.float32, jnp.bfloat16
    vmem = pl.BlockSpec(memory_space=pltpu.VMEM)
    smem = pl.BlockSpec(memory_space=pltpu.SMEM)
    hbm = pl.BlockSpec(memory_space=pl.ANY)
    out_shape = (
        jax.ShapeDtypeStruct((width, width), bf16),
        jax.ShapeDtypeStruct((width, width), f32),
        jax.ShapeDtypeStruct((MATVECS, MATVECS), f32),
    )
    results = pl.pallas_call(
        functools.partial(kernel, segs, secs),
        name="davidson",
        out_shape=out_shape,
        in_specs=[smem, smem, hbm, hbm, hbm, hbm, vmem, hbm],
        out_specs=(vmem, vmem, vmem),
        scratch_shapes=[
            pltpu.VMEM((channels, width, width), bf16),
            pltpu.VMEM((channels, width, width), bf16),
            pltpu.VMEM((width, width), bf16),
            pltpu.VMEM((width, width), f32),
            pltpu.VMEM((width, width), bf16),
            pltpu.VMEM((1, width), bf16),
            pltpu.VMEM((width, width), bf16),
            pltpu.VMEM((width, width), f32),
            pltpu.VMEM((MATVECS + 1, width, width), bf16),
            pltpu.VMEM((channels, ROWS, width), bf16),
            pltpu.VMEM((channels + 1, ROWS, COLS), f32),
            pltpu.VMEM((width, width), f32),
            pltpu.VMEM((halos, ROWS, COLS), bf16),
            pltpu.VMEM((halos, ROWS, COLS), bf16),
            pltpu.VMEM((halos, ROWS, COLS), bf16),
            pltpu.VMEM((halos, ROWS, COLS), bf16),
            pltpu.VMEM((MATVECS, secs, 8, 128), f32),
            pltpu.VMEM((24, 128), f32),
            pltpu.VMEM((MATVECS, 8, 128), f32),
            pltpu.VMEM((8, 128), f32),
            pltpu.SMEM((channels,), jnp.int32),
            pltpu.SemaphoreType.DMA((4,)),
            pltpu.SemaphoreType.DMA((2,)),
            pltpu.SemaphoreType.DMA((2,)),
            pltpu.SemaphoreType.DMA((2, halos)),
            pltpu.SemaphoreType.DMA((2, halos)),
            pltpu.SemaphoreType.DMA((MATVECS,)),
            pltpu.SemaphoreType.DMA((MATVECS,)),
        ],
        compiler_params=pltpu.CompilerParams(
            collective_id=0, has_side_effects=True, vmem_limit_bytes=60 * 1024 * 1024
        ),
    )(
        channel_charge, sector_dims[0, 0], left_env[0, 0], right_env[0, 0],
        left_block[0, 0], right_block[0, 0], inv_sv[0], precond[0, 0],
    )
    following, image, projected = pl.pallas_call(
        finish, name="finish", out_shape=out_shape,
        in_specs=[vmem] * 3, out_specs=(vmem, vmem, vmem),
    )(*results)
    return following[None, None], image[None, None], projected[None]


def solution(mesh):
    in_specs = (
        P("seg", "sec", None, None, None),
        P("seg", "sec", None, None, None),
        P("seg", "sec", None, None),
        P("seg", "sec", None, None),
        P("seg", "sec", None),
        P("seg", "sec", None, None),
        P("seg", "sec", None),
        P(),
    )
    out_specs = (P("seg", "sec", None, None), P("seg", "sec", None, None), P("seg", None, None))
    return jax.shard_map(
        per_device, mesh=mesh, in_specs=in_specs, out_specs=out_specs, check_vma=False
    )
```

profile of v0, /device:TPU:0, one launch (start us, length us, event | category | flops | bytes accessed | tf_op | source)
XLA Modules:
  0.0 99.9 jit_solution(5886619679143824239)
XLA Ops:
  0.6 96.7 %davidson.1 = (bf16[512,512]{1,0:T(8,128)(2,1)}, f32[512,512]{1,0:T(8,128)}, f32[4,4]{1,0:T(4,128)}) custom-call(s32[13]{0:T(128)} %charge_ref.1, s32[2]{0:T(128)} %bitcast.16, bf16[13,512,512]{2,1,0:T(8,128)(2,1)} %bitcast.10, bf16[13,512,512]{2,1,0:T(8,128)(2,1)} %bitcast.11, bf16[512,512]{1,0:T(8,128)(2,1)} %bitcast.13, bf16[512,512]{1,0:T(8,128)(2,1)} %bitcast.14, ...), custom_call_target="tpu_custom_call" | custom-call | tf_op jit(solution)/shard_map/davidson/pallas_call | solution.py:404
  97.3 2.6 %finish.1 = (bf16[512,512]{1,0:T(8,128)(2,1)}, f32[512,512]{1,0:T(8,128)}, f32[4,4]{1,0:T(4,128)}) custom-call(bf16[512,512]{1,0:T(8,128)(2,1)} %get-tuple-element.9.next_in, f32[512,512]{1,0:T(8,128)} %get-tuple-element.10.image_in, f32[4,4]{1,0:T(4,128)} %get-tuple-element.11.projected_in), custom_call_target="tpu_custom_call" | custom-call | tf_op jit(solution)/shard_map/finish/pallas_call | solution.py:447
where the time goes:
time: 100 us; the launch traced here: 99.9 us
  Pallas kernels  99.3 us (99%)
    pallas_call x1, Pallas kernels, per_device(): pl.pallas_call(functools.partial(kernel, segs, secs), name='davidson', ou...  96.7 us
    pallas_call x1, Pallas kernels, per_device(): pl.pallas_call(finish, name='finish', out_shape=out_shape, in_specs=[vmem...  2.57 us

commit v1 on v0

v1 whole, which is shorter than its diff:
```python
import functools

import jax
import jax.numpy as jnp
from jax import lax
from jax.experimental import pallas as pl
from jax.experimental.pallas import tpu as pltpu
from jax.sharding import PartitionSpec as P

MATVECS = 4
EPS = 1e-06
ROWS = 128
COLS = 256
CHUNK = 32
BLOCK = 64
LEAD = 3
QUANTITIES = 4 * MATVECS + 4
MESH = pl.DeviceIdType.MESH


def fold(values):
    rows, columns = values.shape
    block = jnp.sum(values.reshape(rows // 8, 8, columns), axis=0)
    total = block[:, :128]
    for at in range(128, columns, 128):
        total = total + block[:, at : at + 128]
    return total


def spread(tile, values):
    rows, columns = values.shape
    parts = []
    for at in range(0, columns, 128):
        part = values[:, at : at + 128].reshape(rows // 8, 8, 128) * tile[None]
        parts.append(part.reshape(rows, 128))
    return jnp.concatenate(parts, axis=1)


def kernel(
    segs, secs,
    charge_ref, dims_ref, left_hbm, right_hbm, block_hbm, other_hbm, inv_ref, precond_hbm,
    next_ref, image_ref, projected_ref,
    left_ref, right_ref, turned_ref, lx_even, lx_odd, block_ref, precond_ref, nb_ref, ninv_ref, scaled_ref, pinv_ref, basis_ref,
    prefix_even, prefix_odd, part_ref, x_ref, image_half, lifted_half, stay_ref, up_out, low_out, up_in, low_in, y_ref, norm_ref, slots_ref, rows_ref,
    tile_ref, alpha_ref, inner_ref, coef_ref, proj_ref, order_ref,
    load_sem, guess_send, guess_recv, halo_send, halo_recv, sum_send, sum_recv,
):
    channels, width, _ = left_ref.shape
    tiles = width // ROWS
    halves = width // COLS
    pieces = tiles * halves
    count = secs * width * width
    f32, bf16 = jnp.float32, jnp.bfloat16
    seg, sec = lax.axis_index("seg"), lax.axis_index("sec")
    seg_before = lax.rem(seg + segs - 1, segs)
    seg_after = lax.rem(seg + 1, segs)

    load_left = pltpu.make_async_copy(left_hbm, left_ref, load_sem.at[0])
    load_right = pltpu.make_async_copy(right_hbm, right_ref, load_sem.at[1])
    load_block = pltpu.make_async_copy(block_hbm, block_ref, load_sem.at[2])
    load_precond = pltpu.make_async_copy(precond_hbm, precond_ref, load_sem.at[3])
    load_precond.start()
    load_block.start()
    load_right.start()
    load_left.start()

    barrier = pltpu.get_barrier_semaphore()
    pl.semaphore_signal(barrier, inc=1, device_id=(seg_before, sec), device_id_type=MESH)
    pl.semaphore_signal(barrier, inc=1, device_id=(seg_after, sec), device_id_type=MESH)
    for offset in range(1, secs):
        peer = lax.rem(sec + offset, secs)
        pl.semaphore_signal(barrier, inc=1, device_id=(seg, peer), device_id_type=MESH)
    pl.semaphore_wait(barrier, secs + 1)

    def remote(src, dst, send, recv, device):
        return pltpu.make_async_remote_copy(
            src_ref=src, dst_ref=dst, send_sem=send, recv_sem=recv,
            device_id=device, device_id_type=MESH,
        )

    send_inv = remote(
        inv_ref, ninv_ref, guess_send.at[0], guess_recv.at[0], (seg_before, sec)
    )
    send_block = [
        remote(
            other_hbm.at[:, pl.ds(h * COLS, COLS)], nb_ref.at[h],
            guess_send.at[1 + h], guess_recv.at[1 + h], (seg_before, sec),
        )
        for h in range(halves)
    ]
    send_inv.start()
    for copy in send_block:
        copy.start()

    keys = []
    for w in range(channels):
        q = charge_ref[w]
        keys.append(jnp.where(q == 1, 0, jnp.where(q == -1, 1, 2)))
    raising = jnp.int32(0)
    moving = jnp.int32(0)
    for w in range(channels):
        raising = raising + jnp.where(keys[w] == 0, 1, 0)
        moving = moving + jnp.where(keys[w] <= 1, 1, 0)
    places = []
    for w in range(channels):
        place = jnp.int32(0)
        for v in range(channels):
            if v < w:
                place = place + jnp.where(keys[v] <= keys[w], 1, 0)
            elif v > w:
                place = place + jnp.where(keys[v] < keys[w], 1, 0)
        places.append(place)
    for i in range(channels):
        who = jnp.int32(0)
        for w in range(channels):
            who = who + jnp.where(places[w] == i, w, 0)
        order_ref[i] = who

    def masked(values, start, left=0):
        row = start + lax.broadcasted_iota(jnp.int32, values.shape, 0)
        column = left + lax.broadcasted_iota(jnp.int32, values.shape, 1)
        inside = (row < dims_ref[0]) & (column < dims_ref[1])
        return jnp.where(inside, values, 0.0)

    rows_ref[...] = jnp.zeros_like(rows_ref)
    proj_ref[...] = jnp.zeros_like(proj_ref)
    alpha_ref[...] = jnp.zeros_like(alpha_ref)
    lx_refs, prefix_refs = (lx_even, lx_odd), (prefix_even, prefix_odd)
    for prefix in prefix_refs:
        prefix[0] = jnp.zeros((ROWS, COLS), f32)

    @pl.loop(0, width // CHUNK)
    def _(c):
        at = pl.ds(pl.multiple_of(c * CHUNK, CHUNK), CHUNK)
        for k in range(MATVECS):
            basis_ref[k, at, :] = jnp.zeros((CHUNK, width), bf16)

    @pl.when(sec == 0)
    def _():
        @pl.loop(0, MATVECS * pieces)
        def _(n):
            up_in[n] = jnp.zeros((ROWS, COLS), bf16)

    @pl.when(sec == secs - 1)
    def _():
        @pl.loop(0, MATVECS * pieces)
        def _(n):
            low_in[n] = jnp.zeros((ROWS, COLS), bf16)

    load_precond.wait()

    @pl.loop(0, width // CHUNK)
    def _(c):
        at = pl.ds(pl.multiple_of(c * CHUNK, CHUNK), CHUNK)
        pinv_ref[at, :] = masked(1.0 / precond_ref[at, :], c * CHUNK)

    send_inv.wait_recv()
    load_block.wait()
    scaled_ref[...] = (
        block_ref[...].astype(f32) * ninv_ref[...].astype(f32)
    ).astype(bf16)

    load_right.wait()

    @pl.loop(0, channels)
    def _(w):
        for at in range(0, width, 128):
            turned_ref[w, :, at : at + 128] = right_ref[w, at : at + 128, :].T

    load_left.wait()

    def sum_copies(r):
        own = slots_ref.at[r, sec]
        return [
            remote(
                own, own, sum_send.at[r], sum_recv.at[r],
                (seg, lax.rem(sec + offset, secs)),
            )
            for offset in range(1, secs)
        ]

    def up_copy(n):
        return remote(
            up_out.at[n], up_in.at[n], halo_send.at[0, n], halo_recv.at[0, n],
            (seg, lax.rem(sec + 1, secs)),
        )

    def low_copy(n):
        return remote(
            low_out.at[n], low_in.at[n], halo_send.at[1, n], halo_recv.at[1, n],
            (seg, lax.rem(sec + secs - 1, secs)),
        )

    def rows_of(t):
        start = t * ROWS
        return pl.ds(start if isinstance(t, int) else pl.multiple_of(start, ROWS), ROWS)

    waiting = []

    def flush():
        while waiting:
            waiting.pop()()

    def first_product(t, lx, vector, inner):
        for w in range(channels):
            if w == LEAD:
                flush()
            lx[w, :, inner] = jnp.dot(
                left_ref[w, rows_of(t), :], vector, preferred_element_type=f32
            ).astype(bf16)

    def second_product(lx, h, inner):
        across = pl.ds(h * COLS, COLS)
        prefix = prefix_refs[h % 2]
        for i in range(channels):
            if i == LEAD:
                flush()
            w = order_ref[i]
            term = jnp.dot(
                lx[w, :, inner], turned_ref[w, inner, across], preferred_element_type=f32
            )
            prefix[i + 1] = prefix[i] + term

    def parts(h):
        prefix = prefix_refs[h % 2]
        first = prefix[raising]
        second = prefix[moving]
        return first, second - first, prefix[channels] - second

    def send(n, t, h, up, low, stay):
        up_out[n] = up.astype(bf16)
        low_out[n] = low.astype(bf16)

        @pl.when(sec < secs - 1)
        def _():
            up_copy(n).start()

        @pl.when(sec > 0)
        def _():
            low_copy(n).start()

        stay_ref[rows_of(t), pl.ds(h * COLS, COLS)] = stay

    def partial_done(s, t, h):
        found = parts(h)
        p = t * halves + h
        if s > 0:
            found = [part_ref[j, p] + value for j, value in enumerate(found)]
        if s < halves - 1:
            for j, value in enumerate(found):
                part_ref[j, p] = value
        else:
            send(p, t, h, *found)

    def done(n, t, h):
        send(n, t, h, *parts(h))

    def start_from_guess():
        norm_ref[...] = jnp.zeros_like(norm_ref)
        for s in range(halves):
            inner = pl.ds(s * COLS, COLS)
            send_block[s].wait_recv()

            @pl.loop(0, tiles)
            def _(t):
                value = masked(
                    jnp.dot(scaled_ref[rows_of(t), :], nb_ref[s], preferred_element_type=f32),
                    t * ROWS, s * COLS,
                )
                x_ref[rows_of(t), inner] = value.astype(bf16)
                norm_ref[...] += fold(value * value)

            @pl.loop(0, tiles, step=2)
            def _(start):
                for lead in range(2):
                    t = start + lead
                    first_product(t, lx_refs[lead], x_ref[:, inner], inner)
                    for h in range(halves):
                        second_product(lx_refs[lead], h, inner)
                        waiting.append(functools.partial(partial_done, s, t, h))
                flush()

    def refresh(rows, across):
        remain = spread(coef_ref[0], image_ref[rows, across])
        remain = remain - spread(coef_ref[1], x_ref[rows, across].astype(f32))
        remain = remain * pinv_ref[rows, across]
        for j in range(MATVECS):
            remain = remain - spread(coef_ref[2 + j], basis_ref[j, rows, across].astype(f32))
        return remain

    def continue_from(k):
        norm = jnp.zeros((8, 128), f32)
        for h in range(halves):
            across = pl.ds(h * COLS, COLS)
            for c in range(width // CHUNK):
                at = pl.ds(c * CHUNK, CHUNK)
                remain = refresh(at, across)
                x_ref[at, across] = remain.astype(bf16)
                norm = norm + fold(remain * remain)
            first_product(0, lx_refs[0], x_ref[:, across], across)
        norm_ref[...] = norm
        for t in range(tiles):
            lx = lx_refs[t % 2]
            if t > 0:
                first_product(t, lx, x_ref[...], slice(None))
            for h in range(halves):
                second_product(lx, h, slice(None))
                waiting.append(functools.partial(done, k * pieces + t * halves + h, t, h))
        flush()

    def put(row, value):
        rows_ref[row : row + 1, :] = jnp.sum(value, axis=0, keepdims=True)

    @pl.loop(0, MATVECS)
    def _(k):
        pl.when(k == 0)(start_from_guess)
        pl.when(k > 0)(functools.partial(continue_from, k))

        def own(c, carry):
            at = pl.ds(pl.multiple_of(c * CHUNK, CHUNK), CHUNK)
            current = x_ref[at, :].astype(f32)
            basis_ref[k, at, :] = x_ref[at, :]
            y_ref[at, :] = (current * pinv_ref[at, :]).astype(bf16)
            lifted = y_ref[at, :].astype(f32)
            new = []
            for j in range(MATVECS):
                vector = basis_ref[j, at, :].astype(f32)
                new.append(fold(vector * current))
                new.append(fold(vector * lifted))
            new.append(fold(lifted * lifted))
            return tuple(a + b for a, b in zip(carry, new))

        zero = jnp.zeros((8, 128), f32)
        mine = lax.fori_loop(0, width // CHUNK, own, (zero,) * (2 * MATVECS + 1))
        for j in range(MATVECS):
            put(2 * MATVECS + j, mine[2 * j])
            put(3 * MATVECS + j, mine[2 * j + 1])
        put(4 * MATVECS + 2, mine[2 * MATVECS])
        put(4 * MATVECS + 3, norm_ref[...])

        carry = (zero,) * (2 * MATVECS + 2)
        for piece in range(pieces):
            t, h = divmod(piece, halves)
            n = k * pieces + piece
            across = pl.ds(h * COLS, COLS)

            @pl.when(sec > 0)
            def _():
                up_copy(n).wait_recv()

            @pl.when(sec < secs - 1)
            def _():
                low_copy(n).wait_recv()

            for c in range(ROWS // BLOCK):
                inner = pl.ds(c * BLOCK, BLOCK)
                at = pl.ds(t * ROWS + c * BLOCK, BLOCK)
                image = stay_ref[at, across] + up_in[n, inner, :].astype(f32)
                image = image + low_in[n, inner, :].astype(f32)
                image_ref[at, across] = image
                lifted_half[at, across] = (image * pinv_ref[at, across]).astype(bf16)
                image_half[at, across] = image.astype(bf16)
                lifted = lifted_half[at, across].astype(f32)
                image = image_half[at, across].astype(f32)
                new = []
                for j in range(MATVECS):
                    vector = basis_ref[j, at, across].astype(f32)
                    new.append(fold(vector * image))
                    new.append(fold(vector * lifted))
                new.append(fold(lifted * lifted))
                new.append(fold(lifted * y_ref[at, across].astype(f32)))
                carry = tuple(a + b for a, b in zip(carry, new))
        for j in range(MATVECS):
            put(j, carry[2 * j])
            put(MATVECS + j, carry[2 * j + 1])
        put(4 * MATVECS, carry[2 * MATVECS])
        put(4 * MATVECS + 1, carry[2 * MATVECS + 1])

        sums = jnp.sum(rows_ref[...], axis=1, keepdims=True)
        high = sums.shape[0]
        diagonal = lax.broadcasted_iota(jnp.int32, (high, 128), 0) == lax.broadcasted_iota(
            jnp.int32, (high, 128), 1
        )
        slots_ref[k, sec] = jnp.sum(jnp.where(diagonal, sums, 0.0), axis=0, keepdims=True)
        for copy in sum_copies(k):
            copy.start()
        arrived = slots_ref.at[k, pl.ds(0, secs - 1)]
        pltpu.make_async_copy(arrived, arrived, sum_recv.at[k]).wait()
        tile = jnp.sum(slots_ref[k], axis=0) * (1.0 / count)
        tile_ref[k] = tile

        lane = lax.broadcasted_iota(jnp.int32, (1, 128), 1)

        def pick(q):
            value = jnp.sum(jnp.where(lane == q, tile, 0.0), axis=1, keepdims=True)
            return jnp.broadcast_to(value, (8, 128))

        alpha = lax.rsqrt(pick(4 * MATVECS + 3) + EPS)
        alpha_ref[k] = alpha
        theta = alpha * alpha * pick(k)
        coef_ref[0] = alpha
        coef_ref[1] = theta * alpha
        across_tile = lax.broadcasted_iota(jnp.int32, (8, 128), 1)
        down_tile = lax.broadcasted_iota(jnp.int32, (8, 128), 0)
        column = jnp.zeros((8, 128), f32)
        for j in range(MATVECS):
            other = jnp.where(k == j, alpha, alpha_ref[j])
            weight = other * alpha * (pick(MATVECS + j) - theta * pick(3 * MATVECS + j))
            inner_ref[j] = weight
            coef_ref[2 + j] = weight * other
            column = jnp.where(down_tile == j, other * alpha * pick(j), column)
        proj_ref[...] = jnp.where(across_tile == k, column, proj_ref[...])

    lane = lax.broadcasted_iota(jnp.int32, (1, 128), 1)

    def entry(i, q):
        value = jnp.sum(jnp.where(lane == q, tile_ref[i], 0.0), axis=1, keepdims=True)
        return jnp.broadcast_to(value, (8, 128))

    last = MATVECS - 1
    theta = alpha_ref[last] * alpha_ref[last] * entry(last, last)
    norm_sq = (
        entry(last, 4 * MATVECS) - 2.0 * theta * entry(last, 4 * MATVECS + 1)
        + theta * theta * entry(last, 4 * MATVECS + 2)
    )
    norm_sq = norm_sq * alpha_ref[last] * alpha_ref[last]
    for i in range(MATVECS):
        inside = coef_ref[2 + i] * alpha_ref[i] * entry(i, 2 * MATVECS + i) - 2.0 * inner_ref[i]
        for j in range(i):
            inside = inside + 2.0 * coef_ref[2 + j] * alpha_ref[i] * entry(i, 2 * MATVECS + j)
        norm_sq = norm_sq + inner_ref[i] * inside
    coef_ref[2 + MATVECS] = lax.rsqrt(jnp.maximum(norm_sq, 0.0) + EPS)

    @pl.loop(0, width // CHUNK)
    def _(c):
        at = pl.ds(pl.multiple_of(c * CHUNK, CHUNK), CHUNK)
        remain = refresh(at, slice(None))
        next_ref[at, :] = spread(coef_ref[2 + MATVECS], remain).astype(bf16)
        image_ref[at, :] = masked(spread(alpha_ref[last], image_ref[at, :]), c * CHUNK)

    projected_ref[...] = proj_ref[:MATVECS, :MATVECS]

    send_inv.wait_send()
    for copy in send_block:
        copy.wait_send()

    @pl.when(sec < secs - 1)
    def _():
        @pl.loop(0, MATVECS * pieces)
        def _(n):
            up_copy(n).wait_send()

    @pl.when(sec > 0)
    def _():
        @pl.loop(0, MATVECS * pieces)
        def _(n):
            low_copy(n).wait_send()

    @pl.loop(0, MATVECS)
    def _(r):
        sent = slots_ref.at[r, pl.ds(0, secs - 1)]
        pltpu.make_async_copy(sent, sent, sum_send.at[r]).wait()


def finish(next_in, image_in, projected_in, next_ref, image_ref, projected_ref, next_held, image_held, projected_held, into, out):
    parts, rows, _ = image_held.shape
    loads, stores = [], []
    for p in range(parts):
        at = pl.ds(p * rows, rows)
        loads.append(pltpu.make_async_copy(image_in.at[at], image_held.at[p], into.at[2 * p]))
        stores.append(pltpu.make_async_copy(image_held.at[p], image_ref.at[at], out.at[2 * p]))
        loads.append(pltpu.make_async_copy(next_in.at[at], next_held.at[p], into.at[2 * p + 1]))
        stores.append(pltpu.make_async_copy(next_held.at[p], next_ref.at[at], out.at[2 * p + 1]))
    loads.append(pltpu.make_async_copy(projected_in, projected_held, into.at[2 * parts]))
    stores.append(pltpu.make_async_copy(projected_held, projected_ref, out.at[2 * parts]))
    for copy in loads:
        copy.start()
    for arrive, leave in zip(loads, stores):
        arrive.wait()
        leave.start()
    for copy in stores:
        copy.wait()


def per_device(
    left_env, right_env, left_block, right_block, inv_sv, precond, sector_dims, channel_charge
):
    segs, secs = lax.axis_size("seg"), lax.axis_size("sec")
    channels, width = left_env.shape[2], left_env.shape[-1]
    pieces = (width // ROWS) * (width // COLS)
    halos = MATVECS * pieces
    f32, bf16 = jnp.float32, jnp.bfloat16
    vmem = pl.BlockSpec(memory_space=pltpu.VMEM)
    smem = pl.BlockSpec(memory_space=pltpu.SMEM)
    hbm = pl.BlockSpec(memory_space=pl.ANY)
    out_shape = (
        jax.ShapeDtypeStruct((width, width), bf16),
        jax.ShapeDtypeStruct((width, width), f32),
        jax.ShapeDtypeStruct((MATVECS, MATVECS), f32),
    )
    results = pl.pallas_call(
        functools.partial(kernel, segs, secs),
        name="davidson",
        out_shape=out_shape,
        in_specs=[smem, smem, hbm, hbm, hbm, hbm, vmem, hbm],
        out_specs=(vmem, vmem, vmem),
        scratch_shapes=[
            pltpu.VMEM((channels, width, width), bf16),
            pltpu.VMEM((channels, width, width), bf16),
            pltpu.VMEM((channels, width, width), bf16),
            pltpu.VMEM((channels, ROWS, width), bf16),
            pltpu.VMEM((channels, ROWS, width), bf16),
            pltpu.VMEM((width, width), bf16),
            pltpu.VMEM((width, width), f32),
            pltpu.VMEM((width // COLS, width, COLS), bf16),
            pltpu.VMEM((1, width), bf16),
            pltpu.VMEM((width, width), bf16),
            pltpu.VMEM((width, width), f32),
            pltpu.VMEM((MATVECS, width, width), bf16),
            pltpu.VMEM((channels + 1, ROWS, COLS), f32),
            pltpu.VMEM((channels + 1, ROWS, COLS), f32),
            pltpu.VMEM((3, pieces, ROWS, COLS), f32),
            pltpu.VMEM((width, width), bf16),
            pltpu.VMEM((width, width), bf16),
            pltpu.VMEM((width, width), bf16),
            pltpu.VMEM((width, width), f32),
            pltpu.VMEM((halos, ROWS, COLS), bf16),
            pltpu.VMEM((halos, ROWS, COLS), bf16),
            pltpu.VMEM((halos, ROWS, COLS), bf16),
            pltpu.VMEM((halos, ROWS, COLS), bf16),
            pltpu.VMEM((width, width), bf16),
            pltpu.VMEM((8, 128), f32),
            pltpu.VMEM((MATVECS, secs, 1, 128), f32),
            pltpu.VMEM((pl.cdiv(QUANTITIES, 8) * 8, 128), f32),
            pltpu.VMEM((MATVECS, 1, 128), f32),
            pltpu.VMEM((MATVECS, 8, 128), f32),
            pltpu.VMEM((MATVECS, 8, 128), f32),
            pltpu.VMEM((MATVECS + 3, 8, 128), f32),
            pltpu.VMEM((8, 128), f32),
            pltpu.SMEM((channels,), jnp.int32),
            pltpu.SemaphoreType.DMA((4,)),
            pltpu.SemaphoreType.DMA((1 + width // COLS,)),
            pltpu.SemaphoreType.DMA((1 + width // COLS,)),
            pltpu.SemaphoreType.DMA((2, halos)),
            pltpu.SemaphoreType.DMA((2, halos)),
            pltpu.SemaphoreType.DMA((MATVECS,)),
            pltpu.SemaphoreType.DMA((MATVECS,)),
        ],
        compiler_params=pltpu.CompilerParams(
            collective_id=0, has_side_effects=True, vmem_limit_bytes=60 * 1024 * 1024
        ),
    )(
        channel_charge, sector_dims[0, 0], left_env[0, 0], right_env[0, 0],
        left_block[0, 0], right_block[0, 0], inv_sv[0], precond[0, 0],
    )
    parts = width // ROWS
    following, image, projected = pl.pallas_call(
        finish, name="finish", out_shape=out_shape,
        in_specs=[hbm] * 3, out_specs=(hbm, hbm, hbm),
        scratch_shapes=[
            pltpu.VMEM((parts, ROWS, width), bf16),
            pltpu.VMEM((parts, ROWS, width), f32),
            pltpu.VMEM((MATVECS, MATVECS), f32),
            pltpu.SemaphoreType.DMA((2 * parts + 1,)),
            pltpu.SemaphoreType.DMA((2 * parts + 1,)),
        ],
    )(*results)
    return following[None, None], image[None, None], projected[None]


def solution(mesh):
    in_specs = (
        P("seg", "sec", None, None, None),
        P("seg", "sec", None, None, None),
        P("seg", "sec", None, None),
        P("seg", "sec", None, None),
        P("seg", "sec", None),
        P("seg", "sec", None, None),
        P("seg", "sec", None),
        P(),
    )
    out_specs = (P("seg", "sec", None, None), P("seg", "sec", None, None), P("seg", None, None))
    return jax.shard_map(
        per_device, mesh=mesh, in_specs=in_specs, out_specs=out_specs, check_vma=False
    )
```

time: 100 us -> 88 us (0.88)
  Pallas kernels: 99.3 us -> 87.1 us
    pallas_call x1, Pallas kernels: 96.7 us -> 84.9 us  [per_device(): pl.pallas_call(functools.partial(kernel, segs, secs), name='davidson', ou...]
where the time goes in v1:
time: 88 us; the launch traced here: 87.8 us
  Pallas kernels  87.1 us (99%)
    pallas_call x1, Pallas kernels, per_device(): pl.pallas_call(functools.partial(kernel, segs, secs), name='davidson', ou...  84.9 us
    pallas_call x1, Pallas kernels, per_device(): pl.pallas_call(finish, name='finish', out_shape=out_shape, in_specs=[hbm]...  2.25 us

profile of v1, /device:TPU:0, one launch (start us, length us, event | category | flops | bytes accessed | tf_op | source)
XLA Modules:
  0.0 87.8 jit_solution(3575408837216228028)
XLA Ops:
  0.6 84.9 %davidson.1 = (bf16[512,512]{1,0:T(8,128)(2,1)}, f32[512,512]{1,0:T(8,128)}, f32[4,4]{1,0:T(4,128)}) custom-call(s32[13]{0:T(128)} %charge_ref.1, s32[2]{0:T(128)} %bitcast.16, bf16[13,512,512]{2,1,0:T(8,128)(2,1)} %bitcast.10, bf16[13,512,512]{2,1,0:T(8,128)(2,1)} %bitcast.11, bf16[512,512]{1,0:T(8,128)(2,1)} %bitcast.13, bf16[512,512]{1,0:T(8,128)(2,1)} %bitcast.14, ...), custom_call_target="tpu_custom_call" | custom-call | tf_op jit(solution)/shard_map/davidson/pallas_call | solution.py:501
  85.5 2.3 %finish.1 = (bf16[512,512]{1,0:T(8,128)(2,1)}, f32[512,512]{1,0:T(8,128)}, f32[4,4]{1,0:T(4,128)}) custom-call(bf16[512,512]{1,0:T(8,128)(2,1)} %get-tuple-element.9.next_in, f32[512,512]{1,0:T(8,128)} %get-tuple-element.10.image_in, f32[4,4]{1,0:T(4,128)} %get-tuple-element.11.projected_in), custom_call_target="tpu_custom_call" | custom-call | tf_op jit(solution)/shard_map/finish/pallas_call | solution.py:557
